TPU v7x, 32 devices: a whole 2x2x4 slice. The times are simulated.
32 devices in a mesh: dp: 16 (over z, x, core), tensor: 2 (over y).
Axes of the slice: x: 2, y: 2, z: 4, core: 2. Of those that a mesh axis runs over, the one named last changes fastest.
Arguments:
- tokens: bfloat16 [4096, 1024], P('dp'), may hold values from -6 to 6
- cotangent: bfloat16 [4096, 1024], P('dp'), may hold values from -6 to 6
- seq_lens: int32 [64], P('dp'), may hold values from 0 to 256, as said below
- layer_norm_gain: float32 [2, 1024], replicated, may hold values from 0.1 to 1.9
- layer_norm_bias: float32 [2, 1024], replicated, may hold values from -2 to 2
- w_qkv: bfloat16 [3, 1024, 1024], P(None, 'dp', 'tensor'), may hold values from -1 to 1
- b_qv: float32 [2, 1024], P(None, 'tensor'), may hold values from -2 to 2
- w_out: bfloat16 [1024, 1024], P('dp', 'tensor'), may hold values from -0.75 to 0.75
- b_out: float32 [1024], replicated, may hold values from -2 to 2
- w_fc1: bfloat16 [1024, 4096], P('dp', 'tensor'), may hold values from -0.1875 to 0.1875
- b_fc1: float32 [4096], P('tensor'), may hold values from -3 to 3
- w_fc2: bfloat16 [1024, 4096], P('dp', 'tensor'), may hold values from -0.09375 to 0.09375
- b_fc2: float32 [1024], replicated, may hold values from -2 to 2
Outputs:
- output: bfloat16 [4096, 1024], P('dp')
- grad_tokens: float32 [4096, 1024], P('dp')
- grad_norm_gain: float32 [2, 1024], replicated
- grad_norm_bias: float32 [2, 1024], replicated
- grad_w_qkv: float32 [3, 1024, 1024], P(None, 'dp', 'tensor')
- grad_b_qv: float32 [2, 1024], P(None, 'tensor')
- grad_w_out: float32 [1024, 1024], P('dp', 'tensor')
- grad_b_out: float32 [1024], replicated
- grad_w_fc1: float32 [1024, 4096], P('dp', 'tensor')
- grad_b_fc1: float32 [4096], P('tensor')
- grad_w_fc2: float32 [1024, 4096], P('dp', 'tensor')
- grad_b_fc2: float32 [1024], replicated
Inputs may be any that keep to these rules, and one draw needn't show every extreme that they name: `seq_lens`: each device's 4 lengths are whole sequences laid one after another from its first row; they sum to at most 256, and some device holds a single sequence of exactly 256 rows. Rows after a device's sequences are padding.
All inputs are finite; a program needn't handle non-finite values.
Results may differ from a plain program's by a relative error of at most 0.014.
Values may be sent and summed in bfloat16 or wider, within the bound.
A program may use at most 128 MiB of HBM per device.

v0:
```python
import jax
import jax.numpy as jnp
from jax import lax
from jax.sharding import PartitionSpec as P

HEAD_DIM = 64
NORM_EPS = 1e-05
GELU_COEF = 0.7978845608028654


def product(spec, left, right):
    return jnp.einsum(spec, left, right, preferred_element_type=jnp.float32)


def seq_masks(lengths, row_count):
    ends = jnp.cumsum(lengths, dtype=jnp.int32)
    places = jnp.arange(row_count, dtype=jnp.int32)
    segment = jnp.sum((places[:, None] >= ends[None, :]).astype(jnp.int32), axis=1)
    allowed = (segment[:, None] == segment[None, :]) & (places[:, None] >= places[None, :])
    live_rows = places < ends[-1]
    return (allowed, live_rows)


def layer_norm_forward(hidden, gain, shift):
    center = hidden - jnp.mean(hidden, axis=-1, keepdims=True)
    inv_std = lax.rsqrt(jnp.mean(center * center, axis=-1, keepdims=True) + NORM_EPS)
    normal_x = center * inv_std
    return (normal_x * gain + shift, normal_x, inv_std)


def layer_norm_backward(grad_out, gain, normal_x, inv_std):
    scaled = grad_out * gain
    return inv_std * (
        scaled
        - jnp.mean(scaled, axis=-1, keepdims=True)
        - normal_x * jnp.mean(scaled * normal_x, axis=-1, keepdims=True)
    )


def gelu_parts(pre_act):
    inner = GELU_COEF * (pre_act + 0.044715 * pre_act * pre_act * pre_act)
    tanh_val = jnp.tanh(inner)
    value = 0.5 * pre_act * (1.0 + tanh_val)
    slope = 0.5 * (1.0 + tanh_val) + 0.5 * pre_act * (1.0 - tanh_val * tanh_val) * GELU_COEF * (
        1.0 + 3.0 * 0.044715 * pre_act * pre_act
    )
    return (value, slope)


def split_heads(matrix):
    return matrix.reshape(matrix.shape[0], matrix.shape[1] // HEAD_DIM, HEAD_DIM)


def head_scores(query, key_rows, allowed):
    scores = product("qhd,khd->hqk", split_heads(query), split_heads(key_rows)) * HEAD_DIM ** (-0.5)
    return jnp.where(allowed[None], scores, -1e30)


def attend(query, key_rows, value, allowed):
    scores = head_scores(query, key_rows, allowed)
    row_max = jnp.max(scores, axis=-1, keepdims=True)
    logsum = row_max + jnp.log(jnp.sum(jnp.exp(scores - row_max), axis=-1, keepdims=True))
    weights = jnp.exp(scores - logsum).astype(jnp.bfloat16)
    mixed = product("hqk,khd->qhd", weights, split_heads(value)).astype(jnp.bfloat16)
    return (mixed.reshape(query.shape[0], -1), logsum)


def attend_back(query, key_rows, value, heads_out, d_heads, logsum, allowed):
    scores = head_scores(query, key_rows, allowed)
    probs = jnp.exp(scores - logsum)
    probs_low = probs.astype(jnp.bfloat16)
    d_split = split_heads(d_heads)
    d_prob = product("qhd,khd->hqk", d_split, split_heads(value))
    delta = jnp.sum(
        d_split.astype(jnp.float32) * split_heads(heads_out).astype(jnp.float32), axis=-1
    )
    d_score = (probs * (d_prob - jnp.transpose(delta)[:, :, None]) * HEAD_DIM ** (-0.5)).astype(
        jnp.bfloat16
    )
    d_query = product("hqk,khd->qhd", d_score, split_heads(key_rows)).astype(jnp.bfloat16)
    d_key = product("hqk,qhd->khd", d_score, split_heads(query)).astype(jnp.bfloat16)
    d_value = product("hqk,qhd->khd", probs_low, d_split).astype(jnp.bfloat16)
    row_count = query.shape[0]
    return (
        d_query.reshape(row_count, -1),
        d_key.reshape(row_count, -1),
        d_value.reshape(row_count, -1),
    )


def sum_tensor(part):
    low = lax.optimization_barrier(part.astype(jnp.bfloat16))
    count = lax.axis_size("tensor")
    if count != 2:
        return lax.psum(low, "tensor").astype(jnp.float32)
    other = lax.ppermute(low, "tensor", [(0, 1), (1, 0)])
    return low.astype(jnp.float32) + other.astype(jnp.float32)


def sum_dp(vectors):
    return lax.psum(vectors, "dp")


def body(
    tokens,
    cotangent,
    seq_lens,
    layer_norm_gain,
    layer_norm_bias,
    w_qkv,
    b_qv,
    w_out,
    b_out,
    w_fc1,
    b_fc1,
    w_fc2,
    b_fc2,
):
    heads_width, hidden_width = (w_out.shape[1], w_fc1.shape[1])
    attn_shards = jnp.concatenate([w_qkv[0], w_qkv[1], w_qkv[2], w_out], axis=1)
    mlp_shards = jnp.concatenate([w_fc1, w_fc2], axis=1)
    attn_full = lax.all_gather(attn_shards, "dp", axis=0, tiled=True)
    mlp_full = lax.all_gather(mlp_shards, "dp", axis=0, tiled=True)
    qkv_full, out_full = (attn_full[:, : 3 * heads_width], attn_full[:, 3 * heads_width :])
    fc1_full, fc2_full = (mlp_full[:, :hidden_width], mlp_full[:, hidden_width:])
    allowed, live_rows = seq_masks(seq_lens, tokens.shape[0])
    input_tokens = tokens.astype(jnp.float32)
    first_normalized, first_centered_scaled, first_inverse_deviation = layer_norm_forward(
        input_tokens, layer_norm_gain[0], layer_norm_bias[0]
    )
    low1 = first_normalized.astype(jnp.bfloat16)
    proj = product("td,dc->tc", low1, qkv_full)
    query = (proj[:, :heads_width] + b_qv[0]).astype(jnp.bfloat16)
    key_rows = proj[:, heads_width : 2 * heads_width].astype(jnp.bfloat16)
    value = (proj[:, 2 * heads_width :] + b_qv[1]).astype(jnp.bfloat16)
    heads_out, logsum = attend(query, key_rows, value, allowed)
    attn_part = product("tc,dc->td", heads_out, out_full)
    attn_mix = sum_tensor(attn_part)
    first_hidden_state = input_tokens + attn_mix + b_out
    second_normalized, second_centered_scaled, second_inverse_deviation = layer_norm_forward(
        first_hidden_state, layer_norm_gain[1], layer_norm_bias[1]
    )
    low2 = second_normalized.astype(jnp.bfloat16)
    pre_act = jnp.dot(low2, fc1_full, preferred_element_type=jnp.float32) + b_fc1
    act, slope = gelu_parts(pre_act)
    act_low = act.astype(jnp.bfloat16)
    mlp_part = product("tf,df->td", act_low, fc2_full)
    mlp_mix = sum_tensor(mlp_part)
    result = first_hidden_state + mlp_mix + b_fc2
    output = jnp.where(live_rows[:, None], result, 0.0).astype(jnp.bfloat16)
    qkv_back, out_back, fc1_back, fc2_back = (qkv_full, out_full, fc1_full, fc2_full)
    grad_y = jnp.where(live_rows[:, None], cotangent, jnp.zeros_like(cotangent))
    flat_output_gradient = grad_y.astype(jnp.float32)
    d_pre = (jnp.dot(grad_y, fc2_back, preferred_element_type=jnp.float32) * slope).astype(
        jnp.bfloat16
    )
    g_fc2 = product("td,tf->df", grad_y, act_low)
    g_bfc2 = jnp.sum(flat_output_gradient, axis=0)
    g_fc1 = product("td,tf->df", low2, d_pre)
    g_mlp = jnp.concatenate([g_fc1.astype(jnp.bfloat16), g_fc2.astype(jnp.bfloat16)], axis=1)
    shard_mlp = lax.psum_scatter(g_mlp, "dp", scatter_dimension=0, tiled=True)
    g_bfc1 = jnp.sum(d_pre.astype(jnp.float32), axis=0)
    d_norm2_part = product("tf,df->td", d_pre, fc1_back)
    second_norm_delta = sum_tensor(d_norm2_part)
    second_gain_gradient = jnp.sum(second_norm_delta * second_centered_scaled, axis=0)
    g_shift2 = jnp.sum(second_norm_delta, axis=0)
    hidden_first_gradient = flat_output_gradient + layer_norm_backward(
        second_norm_delta, layer_norm_gain[1], second_centered_scaled, second_inverse_deviation
    )
    grad_low = hidden_first_gradient.astype(jnp.bfloat16)
    g_out = product("td,tc->dc", grad_low, heads_out)
    g_bout = jnp.sum(hidden_first_gradient, axis=0)
    d_heads = jnp.dot(grad_low, out_back, preferred_element_type=jnp.float32).astype(jnp.bfloat16)
    d_query, d_key, d_value = attend_back(
        query, key_rows, value, heads_out, d_heads, logsum, allowed
    )
    stacked = jnp.concatenate([d_query, d_key, d_value], axis=1)
    g_qkv = product("td,tc->dc", low1, stacked)
    g_attn = jnp.concatenate([g_qkv.astype(jnp.bfloat16), g_out.astype(jnp.bfloat16)], axis=1)
    shard_attn = lax.psum_scatter(g_attn, "dp", scatter_dimension=0, tiled=True)
    g_bqv = jnp.stack(
        [jnp.sum(d_query.astype(jnp.float32), axis=0), jnp.sum(d_value.astype(jnp.float32), axis=0)]
    )
    d_norm1_part = product("tc,dc->td", stacked, qkv_back)
    first_norm_delta = sum_tensor(d_norm1_part)
    first_gain_gradient = jnp.sum(first_norm_delta * first_centered_scaled, axis=0)
    g_shift1 = jnp.sum(first_norm_delta, axis=0)
    input_gradient = hidden_first_gradient + layer_norm_backward(
        first_norm_delta, layer_norm_gain[0], first_centered_scaled, first_inverse_deviation
    )
    shard_attn, shard_mlp = (shard_attn.astype(jnp.float32), shard_mlp.astype(jnp.float32))
    shard_qkv = jnp.stack(
        [shard_attn[:, i * heads_width : (i + 1) * heads_width] for i in range(3)]
    )
    shard_out = shard_attn[:, 3 * heads_width :]
    shard_fc1, shard_fc2 = (shard_mlp[:, :hidden_width], shard_mlp[:, hidden_width:])
    vectors = jnp.concatenate(
        [
            first_gain_gradient,
            second_gain_gradient,
            g_shift1,
            g_shift2,
            g_bqv.reshape(-1),
            g_bout,
            g_bfc1,
            g_bfc2,
        ]
    )
    vectors = sum_dp(vectors)
    width = tokens.shape[1]
    cuts = [2 * width, 4 * width, 4 * width + 2 * heads_width]
    cuts += [cuts[-1] + width, cuts[-1] + width + hidden_width]
    gain_sum, shift_sum, bqv_sum, bout_sum, bfc1_sum, bfc2_sum = jnp.split(vectors, cuts)
    gain_sum, shift_sum = (gain_sum.reshape(2, width), shift_sum.reshape(2, width))
    bqv_sum = bqv_sum.reshape(2, heads_width)
    return (
        output,
        input_gradient,
        gain_sum,
        shift_sum,
        shard_qkv,
        bqv_sum,
        shard_out,
        bout_sum,
        shard_fc1,
        bfc1_sum,
        shard_fc2,
        bfc2_sum,
    )


def solution(mesh):
    in_specs = (
        P("dp", None),
        P("dp", None),
        P("dp"),
        P(),
        P(),
        P(None, "dp", "tensor"),
        P(None, "tensor"),
        P("dp", "tensor"),
        P(),
        P("dp", "tensor"),
        P("tensor"),
        P("dp", "tensor"),
        P(),
    )
    out_specs = (
        P("dp", None),
        P("dp", None),
        P(),
        P(),
        P(None, "dp", "tensor"),
        P(None, "tensor"),
        P("dp", "tensor"),
        P(),
        P("dp", "tensor"),
        P("tensor"),
        P("dp", "tensor"),
        P(),
    )
    return jax.shard_map(body, mesh=mesh, in_specs=in_specs, out_specs=out_specs, check_vma=False)
```

profile of v0, /device:TPU:0, one launch (start us, length us, event | category | flops | bytes accessed | tf_op | source)
XLA Modules:
  0.0 374.8 jit_solution(1021533827294372795)
XLA Ops:
  7.3 1.0 slice_bitcast_fusion.5
  8.2 1.6 pad_maximum_fusion.7
  9.9 1.9 pad_maximum_fusion.3
  11.8 0.2 reduce-window.4
  12.1 0.1 convert_reduce_fusion.1
  12.2 0.3 fusion.49
  12.7 51.2 %all-gather.3.cloned.1.call-done = bf16[1024,2048]{1,0:T(8,128)(2,1)} async-done(((bf16[64,2048]{1,0:T(8,128)(2,1)}), bf16[1024,2048]{1,0:T(8,128)(2,1)}) %all-gather.3.cloned.1.call-update) | async-done | bytes 4194320 | tf_op jit(solution)/shard_map/all_gather | solution.py:122
  63.9 3.0 fusion.10
  67.0 0.1 copy.49
  67.5 0.5 fusion.79
  68.0 0.3 exponential_reduce_fusion
  68.4 0.5 convolution_convert_fusion.9
  68.8 1.8 convolution_convert_fusion.4
  70.7 1.5 collective-permute-start
  72.2 0.6 slice.97
  72.8 0.7 iota_compare_fusion.2
  73.5 11.3 %collective-permute-done = bf16[256,1024]{1,0:T(8,128)(2,1)S(1)} collective-permute-done((bf16[256,1024]{1,0:T(8,128)(2,1)S(1)}, bf16[256,1024]{1,0:T(8,128)(2,1)S(1)}, u32[]{:S(2)}, u32[]{:S(2)}) %collective-permute-start) | collective-permute-done | bytes 524320 | tf_op jit(solution)/shard_map/ppermute | solution.py:96
  84.8 0.3 fusion.71
  85.1 0.3 multiply_reduce_fusion.2
  85.4 54.1 %all-gather.5.cloned.1.call-done = bf16[1024,4096]{1,0:T(8,128)(2,1)} async-done(((bf16[64,4096]{1,0:T(8,128)(2,1)}), bf16[1024,4096]{1,0:T(8,128)(2,1)}) %all-gather.5.cloned.1.call-update) | async-done | bytes 8388624 | tf_op jit(solution)/shard_map/all_gather | solution.py:123
  139.5 3.7 fusion.12
  143.2 1.1 copy-done.25
  144.3 2.3 convert_reduce_fusion
  146.6 1.4 fusion.30
  148.0 1.5 collective-permute-start.2
  149.6 1.5 fusion.33
  151.1 0.6 collective-permute-start.1
  151.7 11.2 %collective-permute-done.2 = bf16[256,1024]{1,0:T(8,128)(2,1)S(1)} collective-permute-done((bf16[256,1024]{1,0:T(8,128)(2,1)S(1)}, bf16[256,1024]{1,0:T(8,128)(2,1)S(1)}, u32[]{:S(2)}, u32[]{:S(2)}) %collective-permute-start.2) | collective-permute-done | bytes 524320 | tf_op jit(solution)/shard_map/ppermute | solution.py:96
  162.9 0.6 multiply_reduce_fusion
  163.5 9.9 %collective-permute-done.1 = bf16[256,1024]{1,0:T(8,128)(2,1)S(1)} collective-permute-done((bf16[256,1024]{1,0:T(8,128)(2,1)S(1)}, bf16[256,1024]{1,0:T(8,128)(2,1)S(1)}, u32[]{:S(2)}, u32[]{:S(2)}) %collective-permute-start.1) | collective-permute-done | bytes 524320 | tf_op jit(solution)/shard_map/ppermute | solution.py:96
  173.4 1.6 fusion.70
  175.0 1.0 copy-done
  176.0 2.4 convolution_convert_fusion.8
  178.3 1.1 copy.52
  179.4 1.1 multiply_reduce_fusion.3
  180.5 0.7 convert_reduce_fusion.3
  181.2 0.7 multiply_convert_fusion
  181.9 0.3 copy-done.12
  182.2 0.4 convolution_convert_fusion.6
  182.7 0.4 convert_reduce_fusion.4
  183.1 0.4 copy-done.1
  183.5 0.5 convolution_convert_fusion.3
  184.0 1.2 convolution_convert_fusion
  185.2 2.6 pad_maximum_fusion.1
  187.9 4.7 %convolution_convert_fusion.2 = bf16[1024,2048]{1,0:T(8,128)(2,1)} fusion(bf16[256,2048]{1,0:T(8,128)(2,1)} %copy-done.13, f32[256,1024]{1,0:T(8,128)S(1)} %get-tuple-element.23, f32[1024]{0:T(1024)S(1)} %bitcast.80, f32[1024]{0:T(1024)S(1)} %bitcast.78, f32[256]{0:T(256)S(1)} %add_rsqrt_fusion, f32[256]{0:T(256)S(1)} %broadcast_multiply_fusion.4), kind=kOutput, calls=%fused_computation.4 | convolution fusion | flops 1077149696 | bytes 6301696 | tf_op jit(solution)/shard_map/td,tf->df/dot_general | solution.py:12
  192.7 3.4 convolution_convert_fusion.1
  196.1 8.3 %pad_maximum_fusion = bf16[1024,4096]{1,0:T(8,128)(2,1)} fusion(bf16[1024,2048]{1,0:T(8,128)(2,1)} %convolution_convert_fusion.1, bf16[1024,2048]{1,0:T(8,128)(2,1)} %convolution_convert_fusion.2), kind=kLoop, calls=%fused_computation | loop fusion | flops 16777216 | bytes 16777216 | tf_op jit(solution)/shard_map/concatenate | solution.py:160
  204.4 0.9 copy-done.17
  205.4 3.0 fusion.27
  208.4 1.5 collective-permute-start.3
  210.2 11.6 %collective-permute-done.3 = bf16[256,1024]{1,0:T(8,128)(2,1)S(1)} collective-permute-done((bf16[256,1024]{1,0:T(8,128)(2,1)S(1)}, bf16[256,1024]{1,0:T(8,128)(2,1)S(1)}, u32[]{:S(2)}, u32[]{:S(2)}) %collective-permute-start.3) | collective-permute-done | bytes 524320 | tf_op jit(solution)/shard_map/ppermute | solution.py:96
  221.8 0.6 fusion.48
  222.5 58.6 %psum.7 = f32[9216]{0:T(1024)S(1)} all-reduce(f32[9216]{0:T(1024)S(1)} %constant_dynamic-update-slice_fusion), channel_id=1, replica_groups=mesh['dp'=16,'tensor'=2] {'dp'}, use_global_device_ids=true, to_apply=%region_22.23 | all-reduce | flops 9216 | bytes 73728 | tf_op jit(solution)/shard_map/psum | solution.py:101
  281.0 0.6 fusion.74
  281.6 0.6 split.29
  282.2 0.6 fusion.75
  282.8 0.6 split.27
  283.4 0.6 split.25
  284.1 1.4 fusion.47
  285.5 1.5 slice.130
  287.0 1.0 convert_element_type.180
  288.0 0.8 pad_maximum_fusion.4
  288.8 77.4 %reduce-scatter.5.cloned.1.call-done = bf16[64,4096]{1,0:T(8,128)(2,1)} async-done(((bf16[1024,4096]{1,0:T(8,128)(2,1)}), bf16[64,4096]{1,0:T(8,128)(2,1)}) %reduce-scatter.5.cloned.1.call-update) | async-done | bytes 524304 | tf_op jit(solution)/shard_map/reduce_scatter | solution.py:161
  366.1 2.1 fusion.73
  (94 shorter events, 1.4 us)
Async XLA Ops:
  7.2 4.6 %copy-start.27 = (s32[4]{0:T(128)S(1)}, s32[4]{0:T(128)}, u32[]{:S(2)}) copy-start(s32[4]{0:T(128)} %param.15) | copy-start | bytes 52
  7.2 4.9 %copy-start.2 = (bf16[256,1024]{1,0:T(8,128)(2,1)S(1)}, bf16[256,1024]{1,0:T(8,128)(2,1)}, u32[]{:S(2)}) copy-start(bf16[256,1024]{1,0:T(8,128)(2,1)} %param.13) | copy-start | bytes 1572868
  7.2 5.3 %copy-start.24 = (f32[2,512]{1,0:T(2,128)S(1)}, f32[2,512]{1,0:T(2,128)}, u32[]{:S(2)}) copy-start(f32[2,512]{1,0:T(2,128)} %param.19) | copy-start | bytes 12292
  7.2 5.4 %copy-start.20 = (f32[2,1024]{1,0:T(2,128)S(1)}, f32[2,1024]{1,0:T(2,128)}, u32[]{:S(2)}) copy-start(f32[2,1024]{1,0:T(2,128)} %param.16) | copy-start | bytes 24580
  7.2 5.4 %copy-start.21 = (f32[2,1024]{1,0:T(2,128)S(1)}, f32[2,1024]{1,0:T(2,128)}, u32[]{:S(2)}) copy-start(f32[2,1024]{1,0:T(2,128)} %param.17) | copy-start | bytes 24580
  7.2 56.7 %all-gather.3.cloned.1.call-start = ((), (), s32[]{:S(2)}) async-start(), calls=%async_computation.2 | async-start | bytes 4456448 | tf_op jit(solution)/shard_map/all_gather | solution.py:122
  9.8 129.7 %all-gather.5.cloned.1.call-start = ((), (), s32[]{:S(2)}) async-start(), calls=%async_computation.3 | async-start | bytes 8912896 | tf_op jit(solution)/shard_map/all_gather | solution.py:123
  11.8 273.7 %reduce-scatter.3.cloned.1.call-start = ((), (), s32[]{:S(2)}) async-start(), calls=%async_computation.4 | async-start | bytes 4456448 | tf_op jit(solution)/shard_map/reduce_scatter | solution.py:180
  67.2 1.1 copy-start.11
  67.3 1.0 copy-start.9
  67.5 0.9 copy-start.5
  68.4 16.5 %copy-start.3 = (bf16[256,1024]{1,0:T(8,128)(2,1)S(1)}, bf16[256,1024]{1,0:T(8,128)(2,1)}, u32[]{:S(2)}) copy-start(bf16[256,1024]{1,0:T(8,128)(2,1)} %param.13) | copy-start | bytes 1572868
  68.4 16.4 %copy-start.22 = (f32[1024]{0:T(1024)S(1)}, f32[1024]{0:T(1024)}, u32[]{:S(2)}) copy-start(f32[1024]{0:T(1024)} %param.21) | copy-start | bytes 12292
  68.8 4.6 %copy-start.7 = (bf16[8,64,256]{2,1,0:T(8,128)(2,1)}, bf16[8,64,256]{2,1,0:T(8,128)(2,1)S(1)}, u32[]{:S(2)}) copy-start(bf16[8,64,256]{2,1,0:T(8,128)(2,1)S(1)} %convolution_convert_fusion.9) | copy-start | bytes 786436
  70.7 68.8 %copy-start.26 = (f32[2048]{0:T(1024)S(1)}, f32[2048]{0:T(1024)}, u32[]{:S(2)}) copy-start(f32[2048]{0:T(1024)} %param.23) | copy-start | bytes 24580
  70.7 14.1 %collective-permute-start = (bf16[256,1024]{1,0:T(8,128)(2,1)S(1)}, bf16[256,1024]{1,0:T(8,128)(2,1)S(1)}, u32[]{:S(2)}, u32[]{:S(2)}) collective-permute-start(bf16[256,1024]{1,0:T(8,128)(2,1)S(1)} %convolution_convert_fusion.4), channel_id=1, source_target_pairs={{0,1},{1,0},{2,3},{3,2},{4,5},{5,4},{6,7},{7,6},{8,9},{9,8},{10,11... | collective-permute-start | bytes 1572872 | tf_op jit(solution)/shard_map/ppermute | solution.py:96
  139.5 3.7 copy-start.14
  139.5 4.8 %copy-start.25 = (bf16[1024,4096]{1,0:T(8,128)(2,1)S(1)}, bf16[1024,4096]{1,0:T(8,128)(2,1)}, u32[]{:S(2)}) copy-start(bf16[1024,4096]{1,0:T(8,128)(2,1)} %all-gather.5.cloned.1.call-done) | copy-start | bytes 25165828
  144.3 5.2 %copy-start.28 = (f32[256,2048]{1,0:T(8,128)}, f32[256,2048]{1,0:T(8,128)S(1)}, u32[]{:S(2)}) copy-start(f32[256,2048]{1,0:T(8,128)S(1)} %fusion.12) | copy-start | bytes 6291460
  146.6 1.4 copy-start.13
  148.0 14.9 %collective-permute-start.2 = (bf16[256,1024]{1,0:T(8,128)(2,1)S(1)}, bf16[256,1024]{1,0:T(8,128)(2,1)S(1)}, u32[]{:S(2)}, u32[]{:S(2)}) collective-permute-start(bf16[256,1024]{1,0:T(8,128)(2,1)S(1)} %fusion.30), channel_id=1, source_target_pairs={{0,1},{1,0},{2,3},{3,2},{4,5},{5,4},{6,7},{7,6},{8,9},{9,8},{10,11... | collective-permute-start | bytes 1572872 | tf_op jit(solution)/shard_map/ppermute | solution.py:96
  151.0 22.4 %copy-start.23 = (f32[1024]{0:T(1024)S(1)}, f32[1024]{0:T(1024)}, u32[]{:S(2)}) copy-start(f32[1024]{0:T(1024)} %param.25) | copy-start | bytes 12292
  151.1 22.4 %collective-permute-start.1 = (bf16[256,1024]{1,0:T(8,128)(2,1)S(1)}, bf16[256,1024]{1,0:T(8,128)(2,1)S(1)}, u32[]{:S(2)}, u32[]{:S(2)}) collective-permute-start(bf16[256,1024]{1,0:T(8,128)(2,1)S(1)} %fusion.33), channel_id=1, source_target_pairs={{0,1},{1,0},{2,3},{3,2},{4,5},{5,4},{6,7},{7,6},{8,9},{9,8},{10,11... | collective-permute-start | bytes 1572872 | tf_op jit(solution)/shard_map/ppermute | solution.py:96
  175.0 1.0 copy-start
  179.4 1.8 copy-start.6
  181.2 2.8 copy-start.16
  181.2 1.0 copy-start.12
  181.2 1.5 copy-start.10
  182.2 1.2 copy-start.1
  182.2 1.3 copy-start.8
  182.7 1.3 copy-start.4
  183.5 1.7 copy-start.18
  187.9 4.8 %copy-start.15 = (bf16[256,1024]{1,0:T(8,128)(2,1)S(1)}, bf16[256,1024]{1,0:T(8,128)(2,1)}, u32[]{:S(2)}) copy-start(bf16[256,1024]{1,0:T(8,128)(2,1)} %param.14) | copy-start | bytes 1572868
  187.9 178.3 %reduce-scatter.5.cloned.1.call-start = ((), (), s32[]{:S(2)}) async-start(), calls=%async_computation.5 | async-start | bytes 8912896 | tf_op jit(solution)/shard_map/reduce_scatter | solution.py:161
  187.9 4.7 %copy-start.29 = (f32[256,2048]{1,0:T(8,128)S(1)}, f32[256,2048]{1,0:T(8,128)}, u32[]{:S(2)}) copy-start(f32[256,2048]{1,0:T(8,128)} %copy-done.28) | copy-start | bytes 6291460
  204.3 1.0 copy-start.17
  204.3 1.0 copy-start.19
  208.4 13.3 %collective-permute-start.3 = (bf16[256,1024]{1,0:T(8,128)(2,1)S(1)}, bf16[256,1024]{1,0:T(8,128)(2,1)S(1)}, u32[]{:S(2)}, u32[]{:S(2)}) collective-permute-start(bf16[256,1024]{1,0:T(8,128)(2,1)S(1)} %fusion.27), channel_id=1, source_target_pairs={{0,1},{1,0},{2,3},{3,2},{4,5},{5,4},{6,7},{7,6},{8,9},{9,8},{10,11... | collective-permute-start | bytes 1572872 | tf_op jit(solution)/shard_map/ppermute | solution.py:96
Sparse Core Ops, SparseCore 0:
  10.8 53.0 all-gather.2
  66.6 72.8 all-gather.4
  188.0 71.6 reduce-scatter.2
  263.6 102.4 reduce-scatter.4
where the time goes:
time: 375 us
  waiting for transfers between devices  227 us (61%)
  blocking collectives  58.6 us (16%)
  matrix products  31.9 us (9%)
  other arithmetic  23.8 us (6%)
  between operations  14.4 us (4%)
  local copies, waits for them, and re-layouts  13.9 us (4%)
  starting transfers between devices  5.41 us (1%)
    reduce_scatter x1, waiting for transfers between devices, body(): shard_mlp = lax.psum_scatter(g_mlp, 'dp', scatter_dimension=0, tiled=True)  77.4 us
    psum x1, blocking collectives, sum_dp(): return lax.psum(vectors, 'dp')  58.6 us
    all_gather x1, waiting for transfers between devices, body(): mlp_full = lax.all_gather(mlp_shards, 'dp', axis=0, tiled=True)  54.1 us
    all_gather x1, waiting for transfers between devices, body(): attn_full = lax.all_gather(attn_shards, 'dp', axis=0, tiled=True)  51.2 us
    ppermute x4, waiting for transfers between devices, sum_tensor(): other = lax.ppermute(low, 'tensor', [(0, 1), (1, 0)])  44.1 us
    dot_general x15, matrix products, product(): return jnp.einsum(spec, left, right, preferred_element_type=jnp.float32)  23.6 us
    concatenate x1, other arithmetic, body(): jnp.concatenate([g_fc1.astype(jnp.bfloat16), g_fc2.astype(jnp.bfloat16)],...  8.25 us
  transfers between devices with their start and end apart: 8, of which 7 were waited for; matrix products, arithmetic and copies ran while one was open for 11% of the time, Pallas kernels for 0%

commit v1 on v0

--- a/solution.py
+++ b/solution.py
@@ -119,8 +119,13 @@
     heads_width, hidden_width = (w_out.shape[1], w_fc1.shape[1])
     attn_shards = jnp.concatenate([w_qkv[0], w_qkv[1], w_qkv[2], w_out], axis=1)
     mlp_shards = jnp.concatenate([w_fc1, w_fc2], axis=1)
-    attn_full = lax.all_gather(attn_shards, "dp", axis=0, tiled=True)
-    mlp_full = lax.all_gather(mlp_shards, "dp", axis=0, tiled=True)
+    attn_full, mlp_full = jnp.split(
+        lax.all_gather(
+            jnp.concatenate([attn_shards, mlp_shards], axis=1), "dp", axis=0, tiled=True
+        ),
+        [attn_shards.shape[1]],
+        axis=1,
+    )
     qkv_full, out_full = (attn_full[:, : 3 * heads_width], attn_full[:, 3 * heads_width :])
     fc1_full, fc2_full = (mlp_full[:, :hidden_width], mlp_full[:, hidden_width:])
     allowed, live_rows = seq_masks(seq_lens, tokens.shape[0])

time: 375 us -> 374 us (level)
  local copies, waits for them, and re-layouts: 13.9 us -> 18.3 us
  waiting for transfers between devices: 227 us -> 223 us
    unnamed x68 -> x79, local copies, waits for them, and re-layouts: 4.04 us -> 8.37 us
    all_gather x2 -> x1, waiting for transfers between devices: 105 us -> 102 us  [body(): lax.all_gather(jnp.concatenate([attn_shards, mlp_shards], axis=1), 'dp',...]
  transfers between devices with their start and end apart: 8 -> 7, of which waited for: 7 -> 6; matrix products, arithmetic and copies ran while one was open for 11% -> 9% of each run, Pallas kernels for 0% -> 0%
where the time goes in v1:
time: 374 us
  waiting for transfers between devices  223 us (60%)
  blocking collectives  58.4 us (16%)
  matrix products  33.7 us (9%)
  other arithmetic  20.4 us (5%)
  local copies, waits for them, and re-layouts  18.3 us (5%)
  between operations  14.4 us (4%)
  starting transfers between devices  5.36 us (1%)
    all_gather x1, waiting for transfers between devices, body(): lax.all_gather(jnp.concatenate([attn_shards, mlp_shards], axis=1), 'dp',...  102 us
    reduce_scatter x1, waiting for transfers between devices, body(): shard_mlp = lax.psum_scatter(g_mlp, 'dp', scatter_dimension=0, tiled=True)  78.1 us
    psum x1, blocking collectives, sum_dp(): return lax.psum(vectors, 'dp')  58.4 us
    ppermute x4, waiting for transfers between devices, sum_tensor(): other = lax.ppermute(low, 'tensor', [(0, 1), (1, 0)])  42.5 us
    dot_general x15, matrix products, product(): return jnp.einsum(spec, left, right, preferred_element_type=jnp.float32)  23.6 us
    unnamed x79, local copies, waits for them, and re-layouts  8.37 us
    concatenate x1, other arithmetic, body(): jnp.concatenate([g_fc1.astype(jnp.bfloat16), g_fc2.astype(jnp.bfloat16)],...  8.26 us
  transfers between devices with their start and end apart: 7, of which 6 were waited for; matrix products, arithmetic and copies ran while one was open for 9% of the time, Pallas kernels for 0%

profile of v1, /device:TPU:0, one launch (start us, length us, event | category | flops | bytes accessed | tf_op | source)
XLA Modules:
  0.0 373.6 jit_solution(9063703408491999763)
XLA Ops:
  7.3 0.9 bitcast_dynamic-update-slice_fusion.2
  8.2 0.8 bitcast_dynamic-update-slice_fusion.1
  9.0 0.8 bitcast_dynamic-update-slice_fusion
  9.9 0.8 constant_dynamic-update-slice_fusion.2
  10.7 1.0 constant_dynamic-update-slice_fusion.1
  11.7 1.0 constant_dynamic-update-slice_fusion
  12.7 0.9 copy-done.14
  13.6 0.2 reduce-window.4
  14.0 0.3 fusion.49
  14.5 102.3 %all-gather.2.cloned.1.call-done = bf16[1024,6144]{1,0:T(8,128)(2,1)} async-done(((bf16[64,6144]{1,0:T(8,128)(2,1)}), bf16[1024,6144]{1,0:T(8,128)(2,1)}) %all-gather.2.cloned.1.call-update) | async-done | bytes 12582928 | tf_op jit(solution)/shard_map/all_gather | solution.py:123
  116.9 3.0 fusion.10
  120.5 0.5 fusion.79
  121.0 0.3 exponential_reduce_fusion
  121.3 0.5 convolution_convert_fusion.9
  121.8 1.8 convolution_convert_fusion.4
  123.6 1.5 collective-permute-start
  125.2 0.6 slice.101
  125.8 0.6 iota_compare_fusion.2
  126.4 11.4 %collective-permute-done = bf16[256,1024]{1,0:T(8,128)(2,1)S(1)} collective-permute-done((bf16[256,1024]{1,0:T(8,128)(2,1)S(1)}, bf16[256,1024]{1,0:T(8,128)(2,1)S(1)}, u32[]{:S(2)}, u32[]{:S(2)}) %collective-permute-start) | collective-permute-done | bytes 524320 | tf_op jit(solution)/shard_map/ppermute | solution.py:96
  137.8 0.3 fusion.71
  138.1 0.3 multiply_reduce_fusion.2
  138.4 3.7 fusion.12
  142.2 5.3 %convert_reduce_fusion = (f32[2048]{0:T(1024)S(1)}, bf16[256,2048]{1,0:T(8,128)(2,1)S(1)}) fusion(f32[256,2048]{1,0:T(8,128)S(1)} %fusion.12, bf16[1024,6144]{1,0:T(8,128)(2,1)} %all-gather.2.cloned.1.call-done, bf16[256,1024]{1,0:T(8,128)(2,1)S(1)} %copy-done.15, pred[256]{0:T(512)(128)(4,1)S(1)} %iota_compare_fusion.2), kind=kOutput, calls=%fused_computation.27 | convolution fusion | flops 1085011968 | bytes 7872768 | tf_op jit(solution)/shard_map/dot_general | solution.py:159
  147.6 1.4 fusion.30
  149.0 1.5 collective-permute-start.2
  150.6 1.5 fusion.33
  152.1 0.6 collective-permute-start.1
  152.7 11.2 %collective-permute-done.2 = bf16[256,1024]{1,0:T(8,128)(2,1)S(1)} collective-permute-done((bf16[256,1024]{1,0:T(8,128)(2,1)S(1)}, bf16[256,1024]{1,0:T(8,128)(2,1)S(1)}, u32[]{:S(2)}, u32[]{:S(2)}) %collective-permute-start.2) | collective-permute-done | bytes 524320 | tf_op jit(solution)/shard_map/ppermute | solution.py:96
  163.9 0.6 multiply_reduce_fusion
  164.5 9.1 %collective-permute-done.1 = bf16[256,1024]{1,0:T(8,128)(2,1)S(1)} collective-permute-done((bf16[256,1024]{1,0:T(8,128)(2,1)S(1)}, bf16[256,1024]{1,0:T(8,128)(2,1)S(1)}, u32[]{:S(2)}, u32[]{:S(2)}) %collective-permute-start.1) | collective-permute-done | bytes 524320 | tf_op jit(solution)/shard_map/ppermute | solution.py:96
  173.6 1.6 fusion.70
  175.2 1.0 copy-done
  176.1 1.2 convolution_convert_fusion.8
  177.3 1.1 copy.52
  178.4 1.1 multiply_reduce_fusion.3
  179.5 0.7 convert_reduce_fusion.3
  180.2 0.7 multiply_convert_fusion
  180.9 0.3 copy-done.12
  181.3 0.4 convolution_convert_fusion.6
  181.7 0.4 convert_reduce_fusion.4
  182.1 0.4 copy-done.1
  182.5 0.5 convolution_convert_fusion.3
  183.1 1.2 convolution_convert_fusion
  184.3 2.6 pad_maximum_fusion.1
  187.0 4.8 %convolution_convert_fusion.2 = bf16[1024,2048]{1,0:T(8,128)(2,1)} fusion(bf16[256,2048]{1,0:T(8,128)(2,1)} %copy-done.13, f32[256,1024]{1,0:T(8,128)S(1)} %get-tuple-element.23, f32[1024]{0:T(1024)S(1)} %bitcast.80, f32[1024]{0:T(1024)S(1)} %bitcast.78, f32[256]{0:T(256)S(1)} %add_rsqrt_fusion, f32[256]{0:T(256)S(1)} %broadcast_multiply_fusion.4), kind=kOutput, calls=%fused_computation.4 | convolution fusion | flops 1077149696 | bytes 6301696 | tf_op jit(solution)/shard_map/td,tf->df/dot_general | solution.py:12
  191.7 3.4 convolution_convert_fusion.1
  195.2 8.3 %pad_maximum_fusion = bf16[1024,4096]{1,0:T(8,128)(2,1)} fusion(bf16[1024,2048]{1,0:T(8,128)(2,1)} %convolution_convert_fusion.1, bf16[1024,2048]{1,0:T(8,128)(2,1)} %convolution_convert_fusion.2), kind=kLoop, calls=%fused_computation | loop fusion | flops 16777216 | bytes 16777216 | tf_op jit(solution)/shard_map/concatenate | solution.py:165
  203.4 0.9 copy-done.18
  204.5 3.0 fusion.27
  207.5 1.5 collective-permute-start.3
  209.2 10.8 %collective-permute-done.3 = bf16[256,1024]{1,0:T(8,128)(2,1)S(1)} collective-permute-done((bf16[256,1024]{1,0:T(8,128)(2,1)S(1)}, bf16[256,1024]{1,0:T(8,128)(2,1)S(1)}, u32[]{:S(2)}, u32[]{:S(2)}) %collective-permute-start.3) | collective-permute-done | bytes 524320 | tf_op jit(solution)/shard_map/ppermute | solution.py:96
  220.0 0.6 fusion.48
  220.7 58.4 %psum.7 = f32[9216]{0:T(1024)S(1)} all-reduce(f32[9216]{0:T(1024)S(1)} %constant_dynamic-update-slice_fusion.7), channel_id=1, replica_groups=mesh['dp'=16,'tensor'=2] {'dp'}, use_global_device_ids=true, to_apply=%region_22.23 | all-reduce | flops 9216 | bytes 73728 | tf_op jit(solution)/shard_map/psum | solution.py:101
  279.1 0.6 fusion.74
  279.7 0.6 split.31
  280.3 0.6 fusion.75
  280.9 0.6 split.29
  281.5 0.6 split.27
  282.1 1.4 fusion.47
  283.6 1.5 slice.134
  285.1 1.0 convert_element_type.180
  286.1 0.8 pad_maximum_fusion.3
  286.9 78.1 %reduce-scatter.5.cloned.1.call-done = bf16[64,4096]{1,0:T(8,128)(2,1)} async-done(((bf16[1024,4096]{1,0:T(8,128)(2,1)}), bf16[64,4096]{1,0:T(8,128)(2,1)}) %reduce-scatter.5.cloned.1.call-update) | async-done | bytes 524304 | tf_op jit(solution)/shard_map/reduce_scatter | solution.py:166
  365.0 2.1 fusion.73
  (101 shorter events, 1.8 us)
Async XLA Ops:
  7.2 6.4 %copy-start.27 = (s32[4]{0:T(128)S(1)}, s32[4]{0:T(128)}, u32[]{:S(2)}) copy-start(s32[4]{0:T(128)} %param.15) | copy-start | bytes 52
  7.2 6.7 %copy-start.2 = (bf16[256,1024]{1,0:T(8,128)(2,1)S(1)}, bf16[256,1024]{1,0:T(8,128)(2,1)}, u32[]{:S(2)}) copy-start(bf16[256,1024]{1,0:T(8,128)(2,1)} %param.13) | copy-start | bytes 1572868
  7.2 7.1 %copy-start.25 = (f32[2,512]{1,0:T(2,128)S(1)}, f32[2,512]{1,0:T(2,128)}, u32[]{:S(2)}) copy-start(f32[2,512]{1,0:T(2,128)} %param.19) | copy-start | bytes 12292
  7.2 7.2 %copy-start.21 = (f32[2,1024]{1,0:T(2,128)S(1)}, f32[2,1024]{1,0:T(2,128)}, u32[]{:S(2)}) copy-start(f32[2,1024]{1,0:T(2,128)} %param.16) | copy-start | bytes 24580
  7.2 7.2 %copy-start.22 = (f32[2,1024]{1,0:T(2,128)S(1)}, f32[2,1024]{1,0:T(2,128)}, u32[]{:S(2)}) copy-start(f32[2,1024]{1,0:T(2,128)} %param.17) | copy-start | bytes 24580
  7.2 109.6 %all-gather.2.cloned.1.call-start = ((), (), s32[]{:S(2)}) async-start(), calls=%async_computation.2 | async-start | bytes 13369344 | tf_op jit(solution)/shard_map/all_gather | solution.py:123
  12.6 0.9 copy-start.14
  13.6 270.0 %reduce-scatter.3.cloned.1.call-start = ((), (), s32[]{:S(2)}) async-start(), calls=%async_computation.3 | async-start | bytes 4456448 | tf_op jit(solution)/shard_map/reduce_scatter | solution.py:185
  120.1 1.1 copy-start.11
  120.3 1.0 copy-start.9
  120.4 0.9 copy-start.5
  121.3 16.5 %copy-start.3 = (bf16[256,1024]{1,0:T(8,128)(2,1)S(1)}, bf16[256,1024]{1,0:T(8,128)(2,1)}, u32[]{:S(2)}) copy-start(bf16[256,1024]{1,0:T(8,128)(2,1)} %param.13) | copy-start | bytes 1572868
  121.3 16.5 %copy-start.23 = (f32[1024]{0:T(1024)S(1)}, f32[1024]{0:T(1024)}, u32[]{:S(2)}) copy-start(f32[1024]{0:T(1024)} %param.21) | copy-start | bytes 12292
  121.8 4.6 %copy-start.7 = (bf16[8,64,256]{2,1,0:T(8,128)(2,1)}, bf16[8,64,256]{2,1,0:T(8,128)(2,1)S(1)}, u32[]{:S(2)}) copy-start(bf16[8,64,256]{2,1,0:T(8,128)(2,1)S(1)} %convolution_convert_fusion.9) | copy-start | bytes 786436
  123.6 14.8 %copy-start.26 = (f32[2048]{0:T(1024)S(1)}, f32[2048]{0:T(1024)}, u32[]{:S(2)}) copy-start(f32[2048]{0:T(1024)} %param.23) | copy-start | bytes 24580
  123.6 14.2 %collective-permute-start = (bf16[256,1024]{1,0:T(8,128)(2,1)S(1)}, bf16[256,1024]{1,0:T(8,128)(2,1)S(1)}, u32[]{:S(2)}, u32[]{:S(2)}) collective-permute-start(bf16[256,1024]{1,0:T(8,128)(2,1)S(1)} %convolution_convert_fusion.4), channel_id=1, source_target_pairs={{0,1},{1,0},{2,3},{3,2},{4,5},{5,4},{6,7},{7,6},{8,9},{9,8},{10,11... | collective-permute-start | bytes 1572872 | tf_op jit(solution)/shard_map/ppermute | solution.py:96
  138.4 3.7 copy-start.15
  138.4 9.0 %slice-start = ((s8[12582912]{0:T(1024)(128)(4,1)}), s8[4194304]{0:T(1024)(128)(4,1)S(1)}, s32[]{:S(2)}) async-start(s8[12582912]{0:T(1024)(128)(4,1)} %bitcast.81), calls=%async_computation.5 | async-start | bytes 8388608
  142.1 8.4 %copy-start.28 = (f32[256,2048]{1,0:T(8,128)}, f32[256,2048]{1,0:T(8,128)S(1)}, u32[]{:S(2)}) copy-start(f32[256,2048]{1,0:T(8,128)S(1)} %fusion.12) | copy-start | bytes 6291460
  142.1 5.3 %slice-start.1 = ((s8[12582912]{0:T(1024)(128)(4,1)}), s8[4194304]{0:T(1024)(128)(4,1)S(1)}, s32[]{:S(2)}) async-start(s8[12582912]{0:T(1024)(128)(4,1)} %bitcast.81), calls=%async_computation.6 | async-start | bytes 8388608
  142.2 5.5 %slice-start.2 = ((s8[12582912]{0:T(1024)(128)(4,1)}), s8[4194304]{0:T(1024)(128)(4,1)S(1)}, s32[]{:S(2)}) async-start(s8[12582912]{0:T(1024)(128)(4,1)} %bitcast.81), calls=%async_computation.7 | async-start | bytes 8388608
  147.4 1.6 copy-start.13
  149.0 14.9 %collective-permute-start.2 = (bf16[256,1024]{1,0:T(8,128)(2,1)S(1)}, bf16[256,1024]{1,0:T(8,128)(2,1)S(1)}, u32[]{:S(2)}, u32[]{:S(2)}) collective-permute-start(bf16[256,1024]{1,0:T(8,128)(2,1)S(1)} %fusion.30), channel_id=1, source_target_pairs={{0,1},{1,0},{2,3},{3,2},{4,5},{5,4},{6,7},{7,6},{8,9},{9,8},{10,11... | collective-permute-start | bytes 1572872 | tf_op jit(solution)/shard_map/ppermute | solution.py:96
  152.0 21.5 %copy-start.24 = (f32[1024]{0:T(1024)S(1)}, f32[1024]{0:T(1024)}, u32[]{:S(2)}) copy-start(f32[1024]{0:T(1024)} %param.25) | copy-start | bytes 12292
  152.1 21.5 %collective-permute-start.1 = (bf16[256,1024]{1,0:T(8,128)(2,1)S(1)}, bf16[256,1024]{1,0:T(8,128)(2,1)S(1)}, u32[]{:S(2)}, u32[]{:S(2)}) collective-permute-start(bf16[256,1024]{1,0:T(8,128)(2,1)S(1)} %fusion.33), channel_id=1, source_target_pairs={{0,1},{1,0},{2,3},{3,2},{4,5},{5,4},{6,7},{7,6},{8,9},{9,8},{10,11... | collective-permute-start | bytes 1572872 | tf_op jit(solution)/shard_map/ppermute | solution.py:96
  175.2 1.0 copy-start
  178.4 1.8 copy-start.6
  180.2 2.8 copy-start.17
  180.2 1.0 copy-start.12
  180.2 1.5 copy-start.10
  181.3 1.2 copy-start.1
  181.3 1.3 copy-start.8
  181.7 1.3 copy-start.4
  182.5 1.7 copy-start.19
  186.9 4.8 %copy-start.16 = (bf16[256,1024]{1,0:T(8,128)(2,1)S(1)}, bf16[256,1024]{1,0:T(8,128)(2,1)}, u32[]{:S(2)}) copy-start(bf16[256,1024]{1,0:T(8,128)(2,1)} %param.14) | copy-start | bytes 1572868
  186.9 178.1 %reduce-scatter.5.cloned.1.call-start = ((), (), s32[]{:S(2)}) async-start(), calls=%async_computation.4 | async-start | bytes 8912896 | tf_op jit(solution)/shard_map/reduce_scatter | solution.py:166
  187.0 4.8 %copy-start.29 = (f32[256,2048]{1,0:T(8,128)S(1)}, f32[256,2048]{1,0:T(8,128)}, u32[]{:S(2)}) copy-start(f32[256,2048]{1,0:T(8,128)} %copy-done.28) | copy-start | bytes 6291460
  203.4 1.0 copy-start.18
  203.4 1.0 copy-start.20
  207.5 12.5 %collective-permute-start.3 = (bf16[256,1024]{1,0:T(8,128)(2,1)S(1)}, bf16[256,1024]{1,0:T(8,128)(2,1)S(1)}, u32[]{:S(2)}, u32[]{:S(2)}) collective-permute-start(bf16[256,1024]{1,0:T(8,128)(2,1)S(1)} %fusion.27), channel_id=1, source_target_pairs={{0,1},{1,0},{2,3},{3,2},{4,5},{5,4},{6,7},{7,6},{8,9},{9,8},{10,11... | collective-permute-start | bytes 1572872 | tf_op jit(solution)/shard_map/ppermute | solution.py:96
Sparse Core Ops, SparseCore 0:
  13.7 103.1 all-gather.1
  187.0 71.3 reduce-scatter.2
  262.5 102.4 reduce-scatter.4
